TPU v7x, 128 devices: a whole 4x4x4 slice. The times are simulated.
128 devices in a mesh: bank: 4 (over y_hi, core), gal: 32 (over z, y_lo, x).
Axes of the slice: x: 4, y: 4 (y_hi: 2, y_lo: 2; y = y_hi * 2 + y_lo), z: 4, core: 2. Of those that a mesh axis runs over, the one named last changes fastest.
Arguments:
- querybank: bfloat16 [16384, 512], P(('bank', 'gal')), may hold values from -80 to 80
- gallery: bfloat16 [131072, 512], P('gal'), may hold values from -80 to 80
- test_queries: bfloat16 [2048, 512], P(('bank', 'gal')), may hold values from -80 to 80
Outputs:
- retrieval: float32 [2048, 32, 4096], P(None, 'gal', 'bank')
All inputs are finite; a program needn't handle non-finite values.
Results may differ from a plain program's by a relative error of at most 0.0017.
Values may be sent and summed in bfloat16 or wider, within the bound.
A program may use at most 64 MiB of HBM per device.

v0:
```python
import jax
import jax.numpy as jnp
from jax import lax
from jax.sharding import PartitionSpec as P

inverse_temp = 20.0
epsilon = 1e-06


def unit_rows(values):
    wide = values.astype(jnp.float32)
    return (wide * lax.rsqrt(jnp.sum(wide * wide, axis=-1, keepdims=True) + epsilon)).astype(
        jnp.bfloat16
    )


def exp_sums(piece, clips_t):
    rows = piece.shape[0]
    blocks = piece.reshape(rows // 512, 512, piece.shape[1])

    def one_block(total, block):
        sims = jnp.dot(block, clips_t, preferred_element_type=jnp.float32)
        return (total + jnp.sum(jnp.exp(inverse_temp * sims), axis=0), None)

    start_total = jnp.zeros((clips_t.shape[1],), jnp.float32)
    total, unused = lax.scan(one_block, start_total, blocks)
    return total


def local(querybank, gallery, test_queries):
    clips_t = unit_rows(gallery).T
    captions = unit_rows(querybank)
    tests = unit_rows(test_queries)
    groups = lax.axis_size("bank")
    count = captions.shape[0] * lax.axis_size("gal") * groups
    share = clips_t.shape[1] // groups
    partial_sums = exp_sums(lax.all_gather(captions, "gal", axis=0, tiled=True), clips_t)
    totals = lax.psum(partial_sums, "bank")
    mine = lax.dynamic_slice_in_dim(totals, lax.axis_index("bank") * share, share, 0)
    every_test = lax.all_gather(tests, ("bank", "gal"), axis=0, tiled=True)
    columns = lax.dynamic_slice_in_dim(clips_t, lax.axis_index("bank") * share, share, 1)
    sims = jnp.dot(every_test, columns, preferred_element_type=jnp.float32)
    result = inverse_temp * sims - jnp.log(mine / count)[None, :]
    return result[:, None, :]


def solution(mesh):
    placed = (P(("bank", "gal"), None), P("gal", None), P(("bank", "gal"), None))
    return jax.shard_map(
        local, mesh=mesh, in_specs=placed, out_specs=P(None, "gal", "bank"), check_vma=False
    )
```

profile of v0, /device:TPU:1, one launch (start us, length us, event | category | flops | bytes accessed | tf_op | source)
XLA Modules:
  0.0 500.7 jit_solution(5182620168477035748)
XLA Ops:
  6.5 0.0 all-gather.5.cloned.1.call-start
  6.5 1.0 fusion.6
  7.6 1.6 fusion.7
  9.2 0.0 all-gather.5.cloned.1.call-update
  9.2 0.0 all-gather.3.cloned.1.call-start
  9.3 0.8 fusion.8
  10.1 1.4 fusion.9
  11.5 0.0 all-gather.3.cloned.1.call-update
  11.6 6.3 %copy.4 = bf16[4096,512]{0,1:T(8,128)(2,1)} copy(bf16[4096,512]{1,0:T(8,128)(2,1)} %param.6) | data formatting | bytes 8388608 | tf_op args[1]
  17.9 0.0 copy-start
  17.9 3.2 fusion.3
  21.1 0.2 copy-done
  21.3 2.9 fusion.13
  24.2 2.8 fusion.4
  27.0 122.1 %all-gather.5.cloned.1.call-done = bf16[4096,512]{1,0:T(8,128)(2,1)} async-done(((bf16[128,512]{1,0:T(8,128)(2,1)}), bf16[4096,512]{1,0:T(8,128)(2,1)}) %all-gather.5.cloned.1.call-update) | async-done | bytes 4194320 | tf_op jit(solution)/shard_map/all_gather | solution.py:37
  149.1 38.5 %while.11 = (s32[]{:T(128)}, f32[4096]{0:T(1024)S(1)}, bf16[8,512,512]{2,1,0:T(8,128)(2,1)}, bf16[512,4096]{1,0:T(8,128)(2,1)}, s32[]{:T(128)}, /*index=5*/s32[]{:T(128)}) while((s32[]{:T(128)}, f32[4096]{0:T(1024)S(1)}, bf16[8,512,512]{2,1,0:T(8,128)(2,1)}, bf16[512,4096]{1,0:T(8,128)(2,1)}, s32[]{:T(128)}, ...), condition=%wide.region_5.6_spmd.clone, body=%wide.region_3.5_spmd.clone.sunk | while | flops 2151682048 | bytes 4784219 | solution.py:26
  149.1 4.8 exponential_reduce_fusion.2
  153.9 4.8 exponential_reduce_fusion.2
  158.7 4.8 exponential_reduce_fusion.2
  163.5 4.8 exponential_reduce_fusion.2
  168.4 4.8 exponential_reduce_fusion.2
  173.2 4.8 exponential_reduce_fusion.2
  178.0 4.8 exponential_reduce_fusion.2
  182.8 4.8 exponential_reduce_fusion.2
  187.6 32.3 %psum.7 = f32[4096]{0:T(1024)S(1)} all-reduce(f32[4096]{0:T(1024)S(1)} %get-tuple-element.27), channel_id=1, replica_groups=mesh['bank'=4,'gal'=32] {'bank'}, use_global_device_ids=true, to_apply=%region_6.7 | all-reduce | flops 4096 | bytes 32768 | tf_op jit(solution)/shard_map/psum | solution.py:38
  219.9 253.6 %all-gather.3.cloned.1.call-done = bf16[2048,512]{1,0:T(8,128)(2,1)} async-done(((bf16[16,512]{1,0:T(8,128)(2,1)}), bf16[2048,512]{1,0:T(8,128)(2,1)}) %all-gather.3.cloned.1.call-update) | async-done | bytes 2097168 | tf_op jit(solution)/shard_map/all_gather | solution.py:40
  473.5 4.2 subtract_bitcast_fusion
  477.8 16.1 %copy.5 = f32[2048,1,1024]{2,1,0:T(1,128)} copy(f32[2048,1,1024]{2,0,1:T(8,128)S(1)} %subtract_bitcast_fusion) | data formatting | bytes 16777216 | tf_op jit(solution)/shard_map/broadcast_in_dim | solution.py:44
  (13 shorter events, 0.1 us)
Async XLA Ops:
  6.5 142.6 %all-gather.5.cloned.1.call-start = ((), (), s32[]{:S(2)}) async-start(), calls=%async_computation.1 | async-start | bytes 4325376 | tf_op jit(solution)/shard_map/all_gather | solution.py:37
  9.2 464.3 %all-gather.3.cloned.1.call-start = ((), (), s32[]{:S(2)}) async-start(), calls=%async_computation | async-start | bytes 2113536 | tf_op jit(solution)/shard_map/all_gather | solution.py:40
  17.9 3.4 copy-start
Sparse Core Ops, SparseCore 0:
  9.4 139.7 all-gather.4
  150.8 322.6 all-gather.2
where the time goes:
time: 501 us
  waiting for transfers between devices  376 us (75%)
  matrix products  42.4 us (8%)
  blocking collectives  32.3 us (6%)
  local copies, waits for them, and re-layouts  22.7 us (5%)
  other arithmetic  13.9 us (3%)
  between operations  13.5 us (3%)
    all_gather x1, waiting for transfers between devices, local(): every_test = lax.all_gather(tests, ('bank', 'gal'), axis=0, tiled=True)  254 us
    all_gather x1, waiting for transfers between devices, local(): lax.all_gather(captions, 'gal', axis=0, tiled=True)  122 us
    dot_general x8, matrix products, one_block(): sims = jnp.dot(block, clips_t, preferred_element_type=jnp.float32)  38.2 us
    psum x1, blocking collectives, local(): totals = lax.psum(partial_sums, 'bank')  32.3 us
    broadcast_in_dim x1, local copies, waits for them, and re-layouts, local(): return result[:, None, :]  16.1 us
  transfers between devices with their start and end apart: 2, of which 2 were waited for; matrix products, arithmetic and copies ran while one was open for 11% of the time, Pallas kernels for 0%

commit v1 on v0

--- a/solution.py
+++ b/solution.py
@@ -5,6 +5,16 @@
 
 inverse_temp = 20.0
 epsilon = 1e-06
+
+
+def stops_all_press(payload, pos_dim):
+    by_rank = []
+    for _ in range(lax.axis_size(("bank", "gal"))):
+        by_rank.append(payload)
+    met_up = jnp.stack(by_rank, axis=0)
+    value_now = lax.all_to_all(met_up, ("bank", "gal"), 0, 0)
+    block_next = jnp.concatenate(value_now, axis=pos_dim)
+    return block_next
 
 
 def unit_rows(values):
@@ -37,7 +47,7 @@
     partial_sums = exp_sums(lax.all_gather(captions, "gal", axis=0, tiled=True), clips_t)
     totals = lax.psum(partial_sums, "bank")
     mine = lax.dynamic_slice_in_dim(totals, lax.axis_index("bank") * share, share, 0)
-    every_test = lax.all_gather(tests, ("bank", "gal"), axis=0, tiled=True)
+    every_test = stops_all_press(tests, 0)
     columns = lax.dynamic_slice_in_dim(clips_t, lax.axis_index("bank") * share, share, 1)
     sims = jnp.dot(every_test, columns, preferred_element_type=jnp.float32)
     result = inverse_temp * sims - jnp.log(mine / count)[None, :]

time: 501 us -> 256 us (0.51)
  waiting for transfers between devices: 376 us -> 119 us
  starting transfers between devices: 0.04 us -> 11.5 us
    all_gather x1 -> x0, waiting for transfers between devices: 254 us -> none  [local(): every_test = lax.all_gather(tests, ('bank', 'gal'), axis=0, tiled=True)]
    all_to_all x0 -> x1, starting transfers between devices: none -> 11.5 us  [stops_all_press(): value_now = lax.all_to_all(met_up, ('bank', 'gal'), 0, 0)]
  transfers between devices with their start and end apart: 2 -> 2, of which waited for: 2 -> 1; matrix products, arithmetic and copies ran while one was open for 11% -> 22% of each run, Pallas kernels for 0% -> 0%
where the time goes in v1:
time: 256 us
  waiting for transfers between devices  119 us (46%)
  matrix products  41.8 us (16%)
  blocking collectives  32.3 us (13%)
  local copies, waits for them, and re-layouts  24.4 us (10%)
  between operations  13.5 us (5%)
  other arithmetic  13.3 us (5%)
  starting transfers between devices  11.5 us (4%)
    all_gather x1, waiting for transfers between devices, local(): lax.all_gather(captions, 'gal', axis=0, tiled=True)  119 us
    dot_general x8, matrix products, one_block(): sims = jnp.dot(block, clips_t, preferred_element_type=jnp.float32)  38.2 us
    psum x1, blocking collectives, local(): totals = lax.psum(partial_sums, 'bank')  32.3 us
    broadcast_in_dim x1, local copies, waits for them, and re-layouts, local(): return result[:, None, :]  16.1 us
    all_to_all x1, starting transfers between devices, stops_all_press(): value_now = lax.all_to_all(met_up, ('bank', 'gal'), 0, 0)  11.5 us
    unnamed x3, local copies, waits for them, and re-layouts  6.58 us
    convert_element_type x3, other arithmetic, unit_rows(): (wide * lax.rsqrt(jnp.sum(wide * wide, axis=-1, keepdims=True) + epsilon)...  5.24 us
  transfers between devices with their start and end apart: 2, of which 1 were waited for; matrix products, arithmetic and copies ran while one was open for 22% of the time, Pallas kernels for 0%

profile of v1, /device:TPU:1, one launch (start us, length us, event | category | flops | bytes accessed | tf_op | source)
XLA Modules:
  0.0 255.7 jit_solution(3991031435777105618)
XLA Ops:
  6.5 0.0 all-gather.2.cloned.1.call-start
  6.5 1.0 fusion.6
  7.6 1.6 fusion.7
  9.2 0.0 all-gather.2.cloned.1.call-update
  9.2 0.8 fusion.8
  10.1 0.8 fusion.9
  10.9 1.7 stack.2
  12.5 11.5 %all-to-all-start = ((bf16[128,16,512]{2,1,0:T(8,128)(2,1)}), bf16[128,16,512]{2,1,0:T(8,128)(2,1)S(1)}, u32[]{:S(2)}, u32[]{:S(2)}) async-start(bf16[128,16,512]{2,1,0:T(8,128)(2,1)} %stack.2), calls=%async_computation | async-start | bytes 4194304 | tf_op jit(solution)/shard_map/all_to_all | solution.py:15
  24.0 6.3 %copy.4 = bf16[4096,512]{0,1:T(8,128)(2,1)} copy(bf16[4096,512]{1,0:T(8,128)(2,1)} %param.6) | data formatting | bytes 8388608 | tf_op args[1]
  30.4 0.0 copy-start
  30.4 3.2 %fusion.3 = f32[4096]{0:T(1024)S(1)} fusion(bf16[4096,512]{0,1:T(8,128)(2,1)} %copy.4), kind=kLoop, calls=%fused_computation.7 | loop fusion | flops 6287360 | bytes 4210688 | tf_op jit(solution)/shard_map/reduce_sum | solution.py:22
  33.6 0.2 copy-done
  33.9 2.9 %fusion.13 = bf16[512,4096]{1,0:T(8,128)(2,1)} fusion(f32[4096]{0:T(1024)S(1)} %add_rsqrt_fusion, bf16[4096,512]{0,1:T(8,128)(2,1)S(1)} %copy-done), kind=kLoop, calls=%fused_computation.24 | loop fusion | flops 6291456 | bytes 8404992 | tf_op jit(solution)/shard_map/transpose | solution.py:41
  36.8 2.8 %fusion.4 = bf16[4096,512]{0,1:T(8,128)(2,1)} fusion(bf16[4096,512]{0,1:T(8,128)(2,1)S(1)} %copy-done, f32[4096]{0:T(1024)S(1)} %add_rsqrt_fusion), kind=kLoop, calls=%fused_computation.8 | loop fusion | flops 6291456 | bytes 8404992 | tf_op jit(solution)/shard_map/convert_element_type | solution.py:22
  39.6 118.7 %all-gather.2.cloned.1.call-done = bf16[4096,512]{1,0:T(8,128)(2,1)} async-done(((bf16[128,512]{1,0:T(8,128)(2,1)}), bf16[4096,512]{1,0:T(8,128)(2,1)}) %all-gather.2.cloned.1.call-update) | async-done | bytes 4194320 | tf_op jit(solution)/shard_map/all_gather | solution.py:47
  158.3 38.5 %while.11 = (s32[]{:T(128)}, f32[4096]{0:T(1024)S(1)}, bf16[8,512,512]{2,1,0:T(8,128)(2,1)}, bf16[512,4096]{1,0:T(8,128)(2,1)}, s32[]{:T(128)}, /*index=5*/s32[]{:T(128)}) while((s32[]{:T(128)}, f32[4096]{0:T(1024)S(1)}, bf16[8,512,512]{2,1,0:T(8,128)(2,1)}, bf16[512,4096]{1,0:T(8,128)(2,1)}, s32[]{:T(128)}, ...), condition=%wide.region_5.6_spmd.clone, body=%wide.region_3.5_spmd.clone.sunk | while | flops 2151682048 | bytes 4784219 | solution.py:36
  158.3 4.8 %exponential_reduce_fusion.2 = f32[4096]{0:T(1024)S(1)} fusion(bf16[512,4096]{1,0:T(8,128)(2,1)} %get-tuple-element.91, bf16[8,512,512]{2,1,0:T(8,128)(2,1)} %get-tuple-element.90, s32[]{:T(128)S(6)} %copy.8), kind=kOutput, calls=%fused_computation.clone.1 | convolution fusion | flops 2151673856 | bytes 4734980 | tf_op jit(solution)/shard_map/while/body/eval_jaxpr/dot_general | solution.py:32
  163.1 4.8 %exponential_reduce_fusion.2 = f32[4096]{0:T(1024)S(1)} fusion(bf16[512,4096]{1,0:T(8,128)(2,1)} %get-tuple-element.91, bf16[8,512,512]{2,1,0:T(8,128)(2,1)} %get-tuple-element.90, s32[]{:T(128)S(6)} %copy.8), kind=kOutput, calls=%fused_computation.clone.1 | convolution fusion | flops 2151673856 | bytes 4734980 | tf_op jit(solution)/shard_map/while/body/eval_jaxpr/dot_general | solution.py:32
  167.9 4.8 %exponential_reduce_fusion.2 = f32[4096]{0:T(1024)S(1)} fusion(bf16[512,4096]{1,0:T(8,128)(2,1)} %get-tuple-element.91, bf16[8,512,512]{2,1,0:T(8,128)(2,1)} %get-tuple-element.90, s32[]{:T(128)S(6)} %copy.8), kind=kOutput, calls=%fused_computation.clone.1 | convolution fusion | flops 2151673856 | bytes 4734980 | tf_op jit(solution)/shard_map/while/body/eval_jaxpr/dot_general | solution.py:32
  172.7 4.8 %exponential_reduce_fusion.2 = f32[4096]{0:T(1024)S(1)} fusion(bf16[512,4096]{1,0:T(8,128)(2,1)} %get-tuple-element.91, bf16[8,512,512]{2,1,0:T(8,128)(2,1)} %get-tuple-element.90, s32[]{:T(128)S(6)} %copy.8), kind=kOutput, calls=%fused_computation.clone.1 | convolution fusion | flops 2151673856 | bytes 4734980 | tf_op jit(solution)/shard_map/while/body/eval_jaxpr/dot_general | solution.py:32
  177.5 4.8 %exponential_reduce_fusion.2 = f32[4096]{0:T(1024)S(1)} fusion(bf16[512,4096]{1,0:T(8,128)(2,1)} %get-tuple-element.91, bf16[8,512,512]{2,1,0:T(8,128)(2,1)} %get-tuple-element.90, s32[]{:T(128)S(6)} %copy.8), kind=kOutput, calls=%fused_computation.clone.1 | convolution fusion | flops 2151673856 | bytes 4734980 | tf_op jit(solution)/shard_map/while/body/eval_jaxpr/dot_general | solution.py:32
  182.3 4.8 %exponential_reduce_fusion.2 = f32[4096]{0:T(1024)S(1)} fusion(bf16[512,4096]{1,0:T(8,128)(2,1)} %get-tuple-element.91, bf16[8,512,512]{2,1,0:T(8,128)(2,1)} %get-tuple-element.90, s32[]{:T(128)S(6)} %copy.8), kind=kOutput, calls=%fused_computation.clone.1 | convolution fusion | flops 2151673856 | bytes 4734980 | tf_op jit(solution)/shard_map/while/body/eval_jaxpr/dot_general | solution.py:32
  187.1 4.8 %exponential_reduce_fusion.2 = f32[4096]{0:T(1024)S(1)} fusion(bf16[512,4096]{1,0:T(8,128)(2,1)} %get-tuple-element.91, bf16[8,512,512]{2,1,0:T(8,128)(2,1)} %get-tuple-element.90, s32[]{:T(128)S(6)} %copy.8), kind=kOutput, calls=%fused_computation.clone.1 | convolution fusion | flops 2151673856 | bytes 4734980 | tf_op jit(solution)/shard_map/while/body/eval_jaxpr/dot_general | solution.py:32
  191.9 4.8 %exponential_reduce_fusion.2 = f32[4096]{0:T(1024)S(1)} fusion(bf16[512,4096]{1,0:T(8,128)(2,1)} %get-tuple-element.91, bf16[8,512,512]{2,1,0:T(8,128)(2,1)} %get-tuple-element.90, s32[]{:T(128)S(6)} %copy.8), kind=kOutput, calls=%fused_computation.clone.1 | convolution fusion | flops 2151673856 | bytes 4734980 | tf_op jit(solution)/shard_map/while/body/eval_jaxpr/dot_general | solution.py:32
  196.7 32.3 %psum.7 = f32[4096]{0:T(1024)S(1)} all-reduce(f32[4096]{0:T(1024)S(1)} %get-tuple-element.27), channel_id=1, replica_groups=mesh['bank'=4,'gal'=32] {'bank'}, use_global_device_ids=true, to_apply=%region_6.7 | all-reduce | flops 4096 | bytes 32768 | tf_op jit(solution)/shard_map/psum | solution.py:48
  229.1 0.0 all-to-all-done
  229.1 3.6 %subtract_bitcast_fusion = f32[2048,1,1024]{2,0,1:T(8,128)S(1)} fusion(bf16[2048,512]{1,0:T(8,128)(2,1)S(1)} %bitcast.15, f32[1024]{0:T(1024)S(1)} %multiply_log_fusion, bf16[4096,512]{0,1:T(8,128)(2,1)} %fusion.4, s32[]{:T(128)S(6)} %select_n.4), kind=kOutput, calls=%fused_computation.9 | convolution fusion | flops 2151677952 | bytes 11538436 | tf_op jit(solution)/shard_map/dot_general | solution.py:52
  232.7 16.1 %copy.5 = f32[2048,1,1024]{2,1,0:T(1,128)} copy(f32[2048,1,1024]{2,0,1:T(8,128)S(1)} %subtract_bitcast_fusion) | data formatting | bytes 16777216 | tf_op jit(solution)/shard_map/broadcast_in_dim | solution.py:54
  (13 shorter events, 0.1 us)
Async XLA Ops:
  6.5 151.7 %all-gather.2.cloned.1.call-start = ((), (), s32[]{:S(2)}) async-start(), calls=%async_computation.1 | async-start | bytes 4325376 | tf_op jit(solution)/shard_map/all_gather | solution.py:47
  12.5 216.5 %all-to-all-start = ((bf16[128,16,512]{2,1,0:T(8,128)(2,1)}), bf16[128,16,512]{2,1,0:T(8,128)(2,1)S(1)}, u32[]{:S(2)}, u32[]{:S(2)}) async-start(bf16[128,16,512]{2,1,0:T(8,128)(2,1)} %stack.2), calls=%async_computation | async-start | bytes 4194304 | tf_op jit(solution)/shard_map/all_to_all | solution.py:15
  30.4 3.5 %copy-start = (bf16[4096,512]{0,1:T(8,128)(2,1)S(1)}, bf16[4096,512]{0,1:T(8,128)(2,1)}, u32[]{:S(2)}) copy-start(bf16[4096,512]{0,1:T(8,128)(2,1)} %copy.4) | copy-start | bytes 12582916
Sparse Core Ops, SparseCore 0:
  9.4 148.8 all-gather.1
